TPU v7x, 32 devices: a whole 2x2x4 slice. The times are simulated.
32 devices in a mesh: mp: 4 (over x, core), seq: 8 (over z, y).
Axes of the slice: x: 2, y: 2, z: 4, core: 2. Of those that a mesh axis runs over, the one named last changes fastest.
Arguments:
- hidden_in: bfloat16 [2048, 5376], P('seq', 'mp'), may hold values from -28 to 28
- gain_in: float32 [5376], replicated, may hold values from 0.3 to 3
- w_query: bfloat16 [5376, 4096], P('seq', 'mp'), may hold values from -0.078125 to 0.078125
- key_weight: bfloat16 [5376, 2048], P('seq', 'mp'), may hold values from -0.078125 to 0.078125
- value_weight: bfloat16 [5376, 2048], P('seq', 'mp'), may hold values from -0.078125 to 0.078125
- gain_query: float32 [128], replicated, may hold values from 0.3 to 3
- gain_key: float32 [128], replicated, may hold values from 0.3 to 3
- start_pos: int32 [1], replicated, may hold values from 1024 to 4095
- cached_key_rows: bfloat16 [1024, 2048], P(None, 'mp'), may hold values from -140 to 140
- cached_value_rows: bfloat16 [1024, 2048], P(None, 'mp'), may hold values from -5 to 5
- w_out: bfloat16 [4096, 5376], P('seq', 'mp'), may hold values from -1.5 to 1.5
- gain_post: float32 [5376], P('mp'), may hold values from 0.3 to 3
Outputs:
- hidden_out: bfloat16 [2048, 5376], P('seq', 'mp')
All inputs are finite; a program needn't handle non-finite values.
Results may differ from a plain program's by a relative error of at most 0.012.
The roundings to bfloat16 on the way count: a program that leaves them out, or rounds other values in their place, can miss the bound.
Values may be sent and summed in bfloat16 or wider, within the bound.
A program may use at most 128 MiB of HBM per device.

v0:
```python
import jax
import jax.numpy as jnp
from jax import lax
from jax.sharding import PartitionSpec as P

MODEL_WIDTH = 5376
WINDOW_LENGTH = 1024
epsilon = 1e-06
query_scale = 168.0 ** (-0.5)
rope_base = 10000.0


def shifted(x, axis, by):
    peers = lax.axis_size(axis)
    pairs = [(i, i + by) for i in range(peers) if 0 <= i + by < peers]
    return lax.ppermute(x, axis, pairs)


def norm_rows(values, gain):
    return values * lax.rsqrt(jnp.mean(values * values, axis=-1, keepdims=True) + epsilon) * gain


def rotate(tensor, positions):
    half_dim = tensor.shape[-1] // 2
    inverse_freq = rope_base ** (
        -(jnp.arange(half_dim, dtype=jnp.float32) * 2.0) / tensor.shape[-1]
    )
    angles = positions.astype(jnp.float32)[:, None, None] * inverse_freq[None, None, :]
    cosine = jnp.cos(angles)
    sine = jnp.sin(angles)
    first = tensor[..., :half_dim]
    second = tensor[..., half_dim:]
    return jnp.concatenate(
        [first * cosine - second * sine, second * cosine + first * sine], axis=-1
    )


def on_device(
    hidden_in,
    gain_in,
    w_query,
    key_weight,
    value_weight,
    gain_query,
    gain_key,
    start_pos,
    cached_key_rows,
    cached_value_rows,
    w_out,
    gain_post,
):
    n_rows = hidden_in.shape[0]
    head_dim = gain_query.shape[0]
    kv_cols = key_weight.shape[1]
    kv_heads = kv_cols // head_dim
    q_heads = w_query.shape[1] // head_dim
    query_group_count = q_heads // kv_heads
    full_rows = lax.all_gather(hidden_in, "mp", axis=1, tiled=True)
    normed_hidden = norm_rows(full_rows.astype(jnp.float32), gain_in).astype(jnp.bfloat16)

    def add_rows(block_rows):
        return jnp.dot(normed_hidden, block_rows, preferred_element_type=jnp.float32)

    keys_raw = add_rows(lax.all_gather(key_weight, "seq", axis=0, tiled=True))
    values_raw = add_rows(lax.all_gather(value_weight, "seq", axis=0, tiled=True))
    query_matrix = add_rows(lax.all_gather(w_query, "seq", axis=0, tiled=True))
    seq_index = lax.axis_index("seq")
    positions = start_pos[0] + seq_index * n_rows + jnp.arange(n_rows, dtype=jnp.int32)
    query_matrix = (
        rotate(norm_rows(query_matrix.reshape(n_rows, q_heads, head_dim), gain_query), positions)
        * query_scale
    ).astype(jnp.bfloat16)
    fresh_key = rotate(
        norm_rows(keys_raw.reshape(n_rows, kv_heads, head_dim), gain_key), positions
    ).astype(jnp.bfloat16)
    fresh = jnp.stack([fresh_key.reshape(n_rows, kv_cols), values_raw.astype(jnp.bfloat16)])
    reach_shards = (WINDOW_LENGTH + n_rows - 1) // n_rows
    reach_rows = reach_shards * n_rows
    pieces = []
    moving = fresh
    for hop_index in range(reach_shards):
        moving = shifted(moving, "seq", 1)
        pieces.insert(0, moving)
    prior = jnp.concatenate(pieces, axis=1)
    front_pad = reach_rows - WINDOW_LENGTH
    cached = jnp.stack([cached_key_rows, cached_value_rows])
    padded = jnp.concatenate(
        [
            jnp.zeros((2, front_pad, kv_cols), cached.dtype),
            cached,
            jnp.zeros((2, reach_rows, kv_cols), cached.dtype),
        ],
        axis=1,
    )
    cache_start = jnp.minimum(seq_index * n_rows, front_pad + WINDOW_LENGTH)
    from_cache = lax.dynamic_slice_in_dim(padded, cache_start, reach_rows, 1)
    prior_rows = jnp.arange(reach_rows, dtype=jnp.int32)
    use_cache = prior_rows < reach_rows - seq_index * n_rows
    prior = jnp.where(use_cache[None, :, None], from_cache, prior)
    window_kv = jnp.concatenate([prior, fresh], axis=1)
    span_rows = reach_rows + n_rows
    key_heads = window_kv[0].reshape(span_rows, kv_heads, head_dim)
    value_heads = window_kv[1].reshape(span_rows, kv_heads, head_dim)
    query_heads = query_matrix.reshape(n_rows, kv_heads, query_group_count, head_dim)
    scores = jnp.einsum(
        "tkgd,skd->kgts", query_heads, key_heads, preferred_element_type=jnp.float32
    )
    query_index = jnp.arange(n_rows, dtype=jnp.int32)[:, None]
    key_index = jnp.arange(span_rows, dtype=jnp.int32)[None, :]
    visible = (key_index > query_index + reach_rows - WINDOW_LENGTH) & (
        key_index <= query_index + reach_rows
    )
    scores = jnp.where(visible, scores, -jnp.inf)
    row_max = jnp.max(scores, axis=-1, keepdims=True)
    probs = jnp.exp(scores - row_max)
    totals = jnp.sum(probs, axis=-1)
    probs_b = probs.astype(jnp.bfloat16)
    summed = jnp.einsum("kgts,skd->tkgd", probs_b, value_heads, preferred_element_type=jnp.float32)
    summed = summed / jnp.transpose(totals, (2, 0, 1))[..., None]
    attn = summed.reshape(n_rows, q_heads * head_dim).astype(jnp.bfloat16)
    all_heads = lax.all_gather(attn, "mp", axis=1, tiled=True)
    projected = jnp.dot(
        all_heads,
        lax.all_gather(w_out, "seq", axis=0, tiled=True),
        preferred_element_type=jnp.float32,
    )
    squares = lax.psum(jnp.sum(projected * projected, axis=-1), "mp")
    scaling = lax.rsqrt(squares / MODEL_WIDTH + epsilon)
    return (hidden_in.astype(jnp.float32) + projected * scaling[:, None] * gain_post).astype(
        jnp.bfloat16
    )


def solution(mesh):
    in_specs = (
        P("seq", "mp"),
        P(),
        P("seq", "mp"),
        P("seq", "mp"),
        P("seq", "mp"),
        P(),
        P(),
        P(),
        P(None, "mp"),
        P(None, "mp"),
        P("seq", "mp"),
        P("mp"),
    )
    out_specs = P("seq", "mp")
    return jax.shard_map(
        on_device, mesh=mesh, in_specs=in_specs, out_specs=out_specs, check_vma=False
    )
```

profile of v0, /device:TPU:0, one launch (start us, length us, event | category | flops | bytes accessed | tf_op | source)
XLA Modules:
  0.0 618.6 jit_solution(16389566803389255011)
XLA Ops:
  6.5 0.7 all-gather.7.cloned.1.call-update
  7.3 0.7 all-gather.9.cloned.1.call-update
  11.2 26.8 %all-gather.7.cloned.1.call-done = bf16[256,5376]{0,1:T(8,128)(2,1)} async-done(((bf16[256,1344]{0,1:T(8,128)(2,1)}), bf16[256,5376]{0,1:T(8,128)(2,1)}) %all-gather.7.cloned.1.call-update) | async-done | bytes 2752528 | tf_op jit(solution)/shard_map/all_gather | solution.py:58
  37.9 2.5 fusion.3
  40.5 89.1 %all-gather.9.cloned.1.call-done = bf16[5376,512]{1,0:T(8,128)(2,1)} async-done(((bf16[672,512]{1,0:T(8,128)(2,1)}), bf16[5376,512]{1,0:T(8,128)(2,1)}) %all-gather.9.cloned.1.call-update) | async-done | bytes 5505040 | tf_op jit(solution)/shard_map/all_gather | solution.py:64
  129.6 7.3 %fusion.32 = f32[256,512]{1,0:T(8,128)} fusion(bf16[5376,512]{1,0:T(8,128)(2,1)} %all-gather.9.cloned.1.call-done, bf16[256,5376]{0,1:T(8,128)(2,1)} %all-gather.7.cloned.1.call-done, f32[5376]{0:T(1024)S(1)} %copy-done.12, f32[256]{0:T(256)S(1)} %add_rsqrt_fusion.3), kind=kOutput, calls=%fused_computation.60 | convolution fusion | flops 1414791168 | bytes 8804352 | tf_op jit(solution)/shard_map/dot_general | solution.py:62
  137.0 1.4 reshape.136
  140.1 79.4 %all-gather.11.cloned.1.call-done = bf16[5376,512]{1,0:T(8,128)(2,1)} async-done(((bf16[672,512]{1,0:T(8,128)(2,1)}), bf16[5376,512]{1,0:T(8,128)(2,1)}) %all-gather.11.cloned.1.call-update) | async-done | bytes 5505040 | tf_op jit(solution)/shard_map/all_gather | solution.py:65
  219.5 5.7 fusion.21
  225.2 0.7 copy-done.7
  226.0 2.6 collective-permute-start
  228.6 21.6 %collective-permute-done = bf16[2,256,512]{2,1,0:T(8,128)(2,1)S(1)} collective-permute-done((bf16[2,256,512]{2,1,0:T(8,128)(2,1)S(1)}, bf16[2,256,512]{2,1,0:T(8,128)(2,1)S(1)}, u32[]{:S(2)}, u32[]{:S(2)}) %collective-permute-start) | collective-permute-done | bytes 524320 | tf_op jit(solution)/shard_map/ppermute | solution.py:16
  250.2 4.4 collective-permute-start.1
  254.6 10.3 %collective-permute-done.1 = bf16[2,256,512]{2,1,0:T(8,128)(2,1)S(1)} collective-permute-done((bf16[2,256,512]{2,1,0:T(8,128)(2,1)S(1)}, bf16[2,256,512]{2,1,0:T(8,128)(2,1)S(1)}, u32[]{:S(2)}, u32[]{:S(2)}) %collective-permute-start.1) | collective-permute-done | bytes 524320 | tf_op jit(solution)/shard_map/ppermute | solution.py:16
  264.9 14.7 %collective-permute-start.2 = (bf16[2,256,512]{2,1,0:T(8,128)(2,1)S(1)}, bf16[2,256,512]{2,1,0:T(8,128)(2,1)S(1)}, u32[]{:S(2)}, u32[]{:S(2)}) collective-permute-start(bf16[2,256,512]{2,1,0:T(8,128)(2,1)S(1)} %collective-permute-done.1), channel_id=1, source_target_pairs={{0,1},{1,2},{2,3},{3,4},{4,5},{5,6},{6,7},{8,9},{9,10},{10,11},{11... | collective-permute-start | bytes 1572872 | tf_op jit(solution)/shard_map/ppermute | solution.py:16
  279.7 6.6 %collective-permute-done.2 = bf16[2,256,512]{2,1,0:T(8,128)(2,1)S(1)} collective-permute-done((bf16[2,256,512]{2,1,0:T(8,128)(2,1)S(1)}, bf16[2,256,512]{2,1,0:T(8,128)(2,1)S(1)}, u32[]{:S(2)}, u32[]{:S(2)}) %collective-permute-start.2) | collective-permute-done | bytes 524320 | tf_op jit(solution)/shard_map/ppermute | solution.py:16
  286.3 20.5 %collective-permute-start.3 = (bf16[2,256,512]{2,1,0:T(8,128)(2,1)S(1)}, bf16[2,256,512]{2,1,0:T(8,128)(2,1)S(1)}, u32[]{:S(2)}, u32[]{:S(2)}) collective-permute-start(bf16[2,256,512]{2,1,0:T(8,128)(2,1)S(1)} %collective-permute-done.2), channel_id=1, source_target_pairs={{0,1},{1,2},{2,3},{3,4},{4,5},{5,6},{6,7},{8,9},{9,10},{10,11},{11... | collective-permute-start | bytes 1572872 | tf_op jit(solution)/shard_map/ppermute | solution.py:16
  307.1 7.0 %collective-permute-done.3 = bf16[2,256,512]{2,1,0:T(8,128)(2,1)S(1)} collective-permute-done((bf16[2,256,512]{2,1,0:T(8,128)(2,1)S(1)}, bf16[2,256,512]{2,1,0:T(8,128)(2,1)S(1)}, u32[]{:S(2)}, u32[]{:S(2)}) %collective-permute-start.3) | collective-permute-done | bytes 524320 | tf_op jit(solution)/shard_map/ppermute | solution.py:16
  314.1 5.9 fusion.14
  320.2 1.3 fusion.34
  321.5 2.7 reshape_squeeze.7
  324.2 1.5 copy.37
  325.6 85.2 %all-gather.13.cloned.1.call-done = bf16[5376,1024]{1,0:T(8,128)(2,1)} async-done(((bf16[672,1024]{1,0:T(8,128)(2,1)}), bf16[5376,1024]{1,0:T(8,128)(2,1)}) %all-gather.13.cloned.1.call-update) | async-done | bytes 11010064 | tf_op jit(solution)/shard_map/all_gather | solution.py:66
  410.9 8.1 %convolution_bitcast_fusion = f32[32,8,8,128]{3,1,2,0:T(8,128)S(1)} fusion(bf16[5376,1024]{1,0:T(8,128)(2,1)} %all-gather.13.cloned.1.call-done, bf16[256,5376]{0,1:T(8,128)(2,1)} %all-gather.7.cloned.1.call-done, f32[5376]{0:T(1024)S(1)} %copy-done.13, f32[256]{0:T(256)S(1)} %add_rsqrt_fusion.3), kind=kOutput, calls=%fused_computation.27 | convolution fusion | flops 2824077312 | bytes 14833664 | tf_op jit(solution)/shard_map/dot_general | solution.py:62
  421.1 1.7 fusion
  422.9 1.8 fusion.1
  424.7 3.3 divide_convert_fusion
  428.0 147.9 %all-gather.17.cloned.1.call-done = bf16[4096,1344]{0,1:T(8,128)(2,1)} async-done(((bf16[512,1344]{0,1:T(8,128)(2,1)}), bf16[4096,1344]{0,1:T(8,128)(2,1)}) %all-gather.17.cloned.1.call-update) | async-done | bytes 11010064 | tf_op jit(solution)/shard_map/all_gather | solution.py:124
  575.9 22.2 %all-gather.15.cloned.1.call-done = bf16[256,4096]{0,1:T(8,128)(2,1)} async-done(((bf16[256,1024]{0,1:T(8,128)(2,1)}), bf16[256,4096]{0,1:T(8,128)(2,1)}) %all-gather.15.cloned.1.call-update) | async-done | bytes 2097168 | tf_op jit(solution)/shard_map/all_gather | solution.py:121
  598.1 6.4 %multiply_reduce_fusion = (f32[256]{0:T(256)S(1)}, f32[256,1344]{0,1:T(8,128)S(1)}) fusion(bf16[4096,1344]{0,1:T(8,128)(2,1)} %all-gather.17.cloned.1.call-done, bf16[256,4096]{0,1:T(8,128)(2,1)} %all-gather.15.cloned.1.call-done), kind=kOutput, calls=%fused_computation.25 | convolution fusion | flops 2819260160 | bytes 14484480 | tf_op jit(solution)/shard_map/dot_general | solution.py:122
  604.6 5.9 psum.7
  610.5 1.2 add_convert_fusion
  (62 shorter events, 6.8 us)
Async XLA Ops:
  6.5 123.1 %copy-start.12 = (f32[5376]{0:T(1024)S(1)}, f32[5376]{0:T(1024)}, u32[]{:S(2)}) copy-start(f32[5376]{0:T(1024)} %param.13) | copy-start | bytes 64516
  6.5 31.4 %all-gather.7.cloned.1.call-start = ((), (), s32[]{:S(2)}) async-start(), calls=%async_computation | async-start | bytes 3440640 | tf_op jit(solution)/shard_map/all_gather | solution.py:58
  7.3 122.4 %all-gather.9.cloned.1.call-start = ((), (), s32[]{:S(2)}) async-start(), calls=%async_computation.1 | async-start | bytes 6193152 | tf_op jit(solution)/shard_map/all_gather | solution.py:64
  8.0 211.5 %all-gather.11.cloned.1.call-start = ((), (), s32[]{:S(2)}) async-start(), calls=%async_computation.2 | async-start | bytes 6193152 | tf_op jit(solution)/shard_map/all_gather | solution.py:65
  8.7 402.1 %all-gather.13.cloned.1.call-start = ((), (), s32[]{:S(2)}) async-start(), calls=%async_computation.3 | async-start | bytes 12386304 | tf_op jit(solution)/shard_map/all_gather | solution.py:66
  9.3 566.6 %all-gather.17.cloned.1.call-start = ((), (), s32[]{:S(2)}) async-start(), calls=%async_computation.5 | async-start | bytes 12386304 | tf_op jit(solution)/shard_map/all_gather | solution.py:124
  9.9 588.2 %all-gather.15.cloned.1.call-start = ((), (), s32[]{:S(2)}) async-start(), calls=%async_computation.4 | async-start | bytes 2621440 | tf_op jit(solution)/shard_map/all_gather | solution.py:121
  11.2 127.9 %copy-start.3 = (f32[256,64]{1,0:T(8,128)}, f32[256,64]{1,0:T(8,128)S(1)}, u32[]{:S(2)}) copy-start(f32[256,64]{1,0:T(8,128)S(1)} %get-tuple-element.11) | copy-start | bytes 196612
  11.2 127.9 %copy-start.5 = (f32[256,64]{1,0:T(8,128)}, f32[256,64]{1,0:T(8,128)S(1)}, u32[]{:S(2)}) copy-start(f32[256,64]{1,0:T(8,128)S(1)} %get-tuple-element.12) | copy-start | bytes 196612
  40.5 98.3 %copy-start.10 = (f32[128]{0:T(128)S(1)}, f32[128]{0:T(128)}, u32[]{:S(2)}) copy-start(f32[128]{0:T(128)} %param.18) | copy-start | bytes 1540
  137.0 82.6 %copy-start = (bf16[256,5376]{0,1:T(8,128)(2,1)S(1)}, bf16[256,5376]{0,1:T(8,128)(2,1)}, u32[]{:S(2)}) copy-start(bf16[256,5376]{0,1:T(8,128)(2,1)} %all-gather.7.cloned.1.call-done) | copy-start | bytes 8257540
  225.2 0.7 copy-start.7
  226.0 94.1 %copy-start.8 = (bf16[1,256,512]{2,1,0:T(8,128)(2,1)S(1)}, bf16[1,256,512]{2,1,0:T(8,128)(2,1)}, u32[]{:S(2)}) copy-start(bf16[1,256,512]{2,1,0:T(8,128)(2,1)} %copy-done.7) | copy-start | bytes 786436
  226.0 24.2 %collective-permute-start = (bf16[2,256,512]{2,1,0:T(8,128)(2,1)S(1)}, bf16[2,256,512]{2,1,0:T(8,128)(2,1)S(1)}, u32[]{:S(2)}, u32[]{:S(2)}) collective-permute-start(bf16[2,256,512]{2,1,0:T(8,128)(2,1)S(1)} %pad_maximum_fusion), channel_id=1, source_target_pairs={{0,1},{1,2},{2,3},{3,4},{4,5},{5,6},{6,7},{8,9},{9,10},{10,11},{11... | collective-permute-start | bytes 1572872 | tf_op jit(solution)/shard_map/ppermute | solution.py:16
  250.2 14.7 %collective-permute-start.1 = (bf16[2,256,512]{2,1,0:T(8,128)(2,1)S(1)}, bf16[2,256,512]{2,1,0:T(8,128)(2,1)S(1)}, u32[]{:S(2)}, u32[]{:S(2)}) collective-permute-start(bf16[2,256,512]{2,1,0:T(8,128)(2,1)S(1)} %collective-permute-done), channel_id=1, source_target_pairs={{0,1},{1,2},{2,3},{3,4},{4,5},{5,6},{6,7},{8,9},{9,10},{10,11},{11... | collective-permute-start | bytes 1572872 | tf_op jit(solution)/shard_map/ppermute | solution.py:16
  264.9 21.4 %collective-permute-start.2 = (bf16[2,256,512]{2,1,0:T(8,128)(2,1)S(1)}, bf16[2,256,512]{2,1,0:T(8,128)(2,1)S(1)}, u32[]{:S(2)}, u32[]{:S(2)}) collective-permute-start(bf16[2,256,512]{2,1,0:T(8,128)(2,1)S(1)} %collective-permute-done.1), channel_id=1, source_target_pairs={{0,1},{1,2},{2,3},{3,4},{4,5},{5,6},{6,7},{8,9},{9,10},{10,11},{11... | collective-permute-start | bytes 1572872 | tf_op jit(solution)/shard_map/ppermute | solution.py:16
  286.3 27.8 %collective-permute-start.3 = (bf16[2,256,512]{2,1,0:T(8,128)(2,1)S(1)}, bf16[2,256,512]{2,1,0:T(8,128)(2,1)S(1)}, u32[]{:S(2)}, u32[]{:S(2)}) collective-permute-start(bf16[2,256,512]{2,1,0:T(8,128)(2,1)S(1)} %collective-permute-done.2), channel_id=1, source_target_pairs={{0,1},{1,2},{2,3},{3,4},{4,5},{5,6},{6,7},{8,9},{9,10},{10,11},{11... | collective-permute-start | bytes 1572872 | tf_op jit(solution)/shard_map/ppermute | solution.py:16
  320.2 90.7 %copy-start.13 = (f32[5376]{0:T(1024)S(1)}, f32[5376]{0:T(1024)}, u32[]{:S(2)}) copy-start(f32[5376]{0:T(1024)} %param.13) | copy-start | bytes 64516
  325.6 94.1 %copy-start.11 = (f32[128]{0:T(128)S(1)}, f32[128]{0:T(128)}, u32[]{:S(2)}) copy-start(f32[128]{0:T(128)} %param.17) | copy-start | bytes 1540
  418.9 1.1 copy-start.4
  419.0 1.1 copy-start.6
  422.9 1.8 copy-start.2
  428.0 182.5 %copy-start.1 = (bf16[256,1344]{0,1:T(8,128)(2,1)S(1)}, bf16[256,1344]{0,1:T(8,128)(2,1)}, u32[]{:S(2)}) copy-start(bf16[256,1344]{0,1:T(8,128)(2,1)} %param.12) | copy-start | bytes 2064388
  428.0 182.5 %copy-start.9 = (f32[1344]{0:T(1024)S(1)}, f32[1344]{0:T(1024)}, u32[]{:S(2)}) copy-start(f32[1344]{0:T(1024)} %param.23) | copy-start | bytes 16132
Sparse Core Ops, SparseCore 0:
  8.9 28.9 all-gather.6
  40.1 89.4 all-gather.8
  131.8 87.6 all-gather.10
  221.5 189.2 all-gather.12
  412.7 163.1 all-gather.16
  577.3 20.7 all-gather.14
where the time goes:
time: 619 us
  waiting for transfers between devices  499 us (81%)
  starting transfers between devices  42.4 us (7%)
  matrix products  32.6 us (5%)
  other arithmetic  15.4 us (2%)
  between operations  14.5 us (2%)
  local copies, waits for them, and re-layouts  8.49 us (1%)
    all_gather x1, waiting for transfers between devices, on_device(): lax.all_gather(w_out, 'seq', axis=0, tiled=True)  148 us
    all_gather x1, waiting for transfers between devices, on_device(): keys_raw = add_rows(lax.all_gather(key_weight, 'seq', axis=0, tiled=True))  89.1 us
    all_gather x1, waiting for transfers between devices, on_device(): query_matrix = add_rows(lax.all_gather(w_query, 'seq', axis=0, tiled=True))  85.2 us
    all_gather x1, waiting for transfers between devices, on_device(): lax.all_gather(value_weight, 'seq', axis=0, tiled=True)  79.4 us
    ppermute x4, waiting for transfers between devices, shifted(): return lax.ppermute(x, axis, pairs)  45.6 us
    ppermute x4, starting transfers between devices, shifted(): return lax.ppermute(x, axis, pairs)  42.2 us
    all_gather x1, waiting for transfers between devices, on_device(): full_rows = lax.all_gather(hidden_in, 'mp', axis=1, tiled=True)  26.8 us
    all_gather x1, waiting for transfers between devices, on_device(): all_heads = lax.all_gather(attn, 'mp', axis=1, tiled=True)  22.2 us
  transfers between devices with their start and end apart: 10, of which 10 were waited for; matrix products, arithmetic and copies ran while one was open for 8% of the time, Pallas kernels for 0%

commit v1 on v0

--- a/solution.py
+++ b/solution.py
@@ -55,7 +55,12 @@
     kv_heads = kv_cols // head_dim
     q_heads = w_query.shape[1] // head_dim
     query_group_count = q_heads // kv_heads
-    full_rows = lax.all_gather(hidden_in, "mp", axis=1, tiled=True)
+    ring = [hidden_in]
+    for hop in range(3):
+        ring.append(lax.ppermute(ring[-1], "mp", [(dev, (dev + 1) % 4) for dev in range(4)]))
+    full_rows = jnp.roll(
+        jnp.concatenate(ring[::-1], axis=1), (lax.axis_index("mp") + 1) * ring[0].shape[1], axis=1
+    )
     normed_hidden = norm_rows(full_rows.astype(jnp.float32), gain_in).astype(jnp.bfloat16)
 
     def add_rows(block_rows):

time: 619 us -> 591 us (0.955)
  waiting for transfers between devices: 499 us -> 466 us
    all_gather x1, waiting for transfers between devices: 89.1 us -> 56.5 us  [on_device(): keys_raw = add_rows(lax.all_gather(key_weight, 'seq', axis=0, tiled=True))]
    ppermute x0 -> x3, waiting for transfers between devices: none -> 30.2 us  [on_device(): lax.ppermute(ring[-1], 'mp', [(dev, (dev + 1) % 4) for dev in range(4)])]
    all_gather x1 -> x0, waiting for transfers between devices: 26.8 us -> none  [on_device(): full_rows = lax.all_gather(hidden_in, 'mp', axis=1, tiled=True)]
  transfers between devices with their start and end apart: 10 -> 12, of which waited for: 10 -> 12; matrix products, arithmetic and copies ran while one was open for 8% -> 9% of each run, Pallas kernels for 0% -> 0%
where the time goes in v1:
time: 591 us
  waiting for transfers between devices  466 us (79%)
  starting transfers between devices  44.1 us (7%)
  matrix products  32.7 us (6%)
  other arithmetic  15.7 us (3%)
  between operations  14.1 us (2%)
  local copies, waits for them, and re-layouts  12.4 us (2%)
    all_gather x1, waiting for transfers between devices, on_device(): lax.all_gather(w_out, 'seq', axis=0, tiled=True)  142 us
    all_gather x1, waiting for transfers between devices, on_device(): query_matrix = add_rows(lax.all_gather(w_query, 'seq', axis=0, tiled=True))  84.6 us
    all_gather x1, waiting for transfers between devices, on_device(): lax.all_gather(value_weight, 'seq', axis=0, tiled=True)  81.4 us
    all_gather x1, waiting for transfers between devices, on_device(): keys_raw = add_rows(lax.all_gather(key_weight, 'seq', axis=0, tiled=True))  56.5 us
    ppermute x4, waiting for transfers between devices, shifted(): return lax.ppermute(x, axis, pairs)  45.8 us
    ppermute x4, starting transfers between devices, shifted(): return lax.ppermute(x, axis, pairs)  43.4 us
    ppermute x3, waiting for transfers between devices, on_device(): lax.ppermute(ring[-1], 'mp', [(dev, (dev + 1) % 4) for dev in range(4)])  30.2 us
    all_gather x1, waiting for transfers between devices, on_device(): all_heads = lax.all_gather(attn, 'mp', axis=1, tiled=True)  22.2 us
  transfers between devices with their start and end apart: 12, of which 12 were waited for; matrix products, arithmetic and copies ran while one was open for 9% of the time, Pallas kernels for 0%

profile of v1, /device:TPU:0, one launch (start us, length us, event | category | flops | bytes accessed | tf_op | source)
XLA Modules:
  0.0 590.6 jit_solution(4013019380662077168)
XLA Ops:
  9.9 10.8 %collective-permute-done = bf16[256,1344]{0,1:T(8,128)(2,1)S(1)} collective-permute-done((bf16[256,1344]{0,1:T(8,128)(2,1)}, bf16[256,1344]{0,1:T(8,128)(2,1)S(1)}, u32[]{:S(2)}, u32[]{:S(2)}) %collective-permute-start) | collective-permute-done | bytes 688160 | tf_op jit(solution)/shard_map/ppermute | solution.py:60
  20.7 10.3 %collective-permute-done.1 = bf16[256,1344]{0,1:T(8,128)(2,1)S(1)} collective-permute-done((bf16[256,1344]{0,1:T(8,128)(2,1)S(1)}, bf16[256,1344]{0,1:T(8,128)(2,1)S(1)}, u32[]{:S(2)}, u32[]{:S(2)}) %collective-permute-start.1) | collective-permute-done | bytes 688160 | tf_op jit(solution)/shard_map/ppermute | solution.py:60
  32.2 9.1 %collective-permute-done.2 = bf16[256,1344]{0,1:T(8,128)(2,1)S(1)} collective-permute-done((bf16[256,1344]{0,1:T(8,128)(2,1)S(1)}, bf16[256,1344]{0,1:T(8,128)(2,1)S(1)}, u32[]{:S(2)}, u32[]{:S(2)}) %collective-permute-start.2) | collective-permute-done | bytes 688160 | tf_op jit(solution)/shard_map/ppermute | solution.py:60
  41.8 2.4 copy-done.1
  45.2 56.5 %all-gather.6.cloned.1.call-done = bf16[5376,512]{1,0:T(8,128)(2,1)} async-done(((bf16[672,512]{1,0:T(8,128)(2,1)}), bf16[5376,512]{1,0:T(8,128)(2,1)}) %all-gather.6.cloned.1.call-update) | async-done | bytes 5505040 | tf_op jit(solution)/shard_map/all_gather | solution.py:69
  101.7 6.5 %fusion.32 = f32[256,512]{1,0:T(8,128)S(1)} fusion(bf16[5376,512]{1,0:T(8,128)(2,1)} %all-gather.6.cloned.1.call-done, f32[5376]{0:T(1024)S(1)} %copy-done.8, f32[256]{0:T(256)S(1)} %add_rsqrt_fusion.3, bf16[256,10752]{0,1:T(8,128)(2,1)} %copy-done.1, s32[]{:T(128)S(6)} %select_n.26), kind=kOutput, calls=%fused_computation.68 | convolution fusion | flops 1414791168 | bytes 8804356 | tf_op jit(solution)/shard_map/dot_general | solution.py:67
  110.2 81.4 %all-gather.8.cloned.1.call-done = bf16[5376,512]{1,0:T(8,128)(2,1)} async-done(((bf16[672,512]{1,0:T(8,128)(2,1)}), bf16[5376,512]{1,0:T(8,128)(2,1)}) %all-gather.8.cloned.1.call-update) | async-done | bytes 5505040 | tf_op jit(solution)/shard_map/all_gather | solution.py:70
  191.6 6.5 %fusion.21 = bf16[1,256,512]{2,1,0:T(8,128)(2,1)S(1)} fusion(bf16[5376,512]{1,0:T(8,128)(2,1)} %all-gather.8.cloned.1.call-done, f32[5376]{0:T(1024)S(1)} %copy-done.8, f32[256]{0:T(256)S(1)} %add_rsqrt_fusion.3, bf16[256,10752]{0,1:T(8,128)(2,1)} %copy-done.1, s32[]{:T(128)S(6)} %select_n.26), kind=kOutput, calls=%fused_computation.32 | convolution fusion | flops 1414922240 | bytes 8542212 | tf_op jit(solution)/shard_map/dot_general | solution.py:67
  198.2 2.5 collective-permute-start.3
  200.7 21.6 %collective-permute-done.3 = bf16[2,256,512]{2,1,0:T(8,128)(2,1)S(1)} collective-permute-done((bf16[2,256,512]{2,1,0:T(8,128)(2,1)S(1)}, bf16[2,256,512]{2,1,0:T(8,128)(2,1)S(1)}, u32[]{:S(2)}, u32[]{:S(2)}) %collective-permute-start.3) | collective-permute-done | bytes 524320 | tf_op jit(solution)/shard_map/ppermute | solution.py:16
  222.3 5.2 collective-permute-start.4
  227.5 9.6 %collective-permute-done.4 = bf16[2,256,512]{2,1,0:T(8,128)(2,1)} collective-permute-done((bf16[2,256,512]{2,1,0:T(8,128)(2,1)S(1)}, bf16[2,256,512]{2,1,0:T(8,128)(2,1)}, u32[]{:S(2)}, u32[]{:S(2)}) %collective-permute-start.4) | collective-permute-done | bytes 524320 | tf_op jit(solution)/shard_map/ppermute | solution.py:16
  237.1 15.3 %collective-permute-start.5 = (bf16[2,256,512]{2,1,0:T(8,128)(2,1)}, bf16[2,256,512]{2,1,0:T(8,128)(2,1)}, u32[]{:S(2)}, u32[]{:S(2)}) collective-permute-start(bf16[2,256,512]{2,1,0:T(8,128)(2,1)} %collective-permute-done.4), channel_id=1, source_target_pairs={{0,1},{1,2},{2,3},{3,4},{4,5},{5,6},{6,7},{8,9},{9,10},{10,11},{11... | collective-permute-start | bytes 1572872 | tf_op jit(solution)/shard_map/ppermute | solution.py:16
  252.3 6.2 %collective-permute-done.5 = bf16[2,256,512]{2,1,0:T(8,128)(2,1)} collective-permute-done((bf16[2,256,512]{2,1,0:T(8,128)(2,1)}, bf16[2,256,512]{2,1,0:T(8,128)(2,1)}, u32[]{:S(2)}, u32[]{:S(2)}) %collective-permute-start.5) | collective-permute-done | bytes 524320 | tf_op jit(solution)/shard_map/ppermute | solution.py:16
  258.5 20.5 %collective-permute-start.6 = (bf16[2,256,512]{2,1,0:T(8,128)(2,1)}, bf16[2,256,512]{2,1,0:T(8,128)(2,1)S(1)}, u32[]{:S(2)}, u32[]{:S(2)}) collective-permute-start(bf16[2,256,512]{2,1,0:T(8,128)(2,1)} %collective-permute-done.5), channel_id=1, source_target_pairs={{0,1},{1,2},{2,3},{3,4},{4,5},{5,6},{6,7},{8,9},{9,10},{10,11},{11... | collective-permute-start | bytes 1572872 | tf_op jit(solution)/shard_map/ppermute | solution.py:16
  279.3 8.5 %collective-permute-done.6 = bf16[2,256,512]{2,1,0:T(8,128)(2,1)S(1)} collective-permute-done((bf16[2,256,512]{2,1,0:T(8,128)(2,1)}, bf16[2,256,512]{2,1,0:T(8,128)(2,1)S(1)}, u32[]{:S(2)}, u32[]{:S(2)}) %collective-permute-start.6) | collective-permute-done | bytes 524320 | tf_op jit(solution)/shard_map/ppermute | solution.py:16
  287.7 5.5 fusion.14
  293.4 1.8 fusion.34
  295.2 2.7 reshape_squeeze.7
  297.9 2.4 copy.37
  300.3 84.6 %all-gather.10.cloned.1.call-done = bf16[5376,1024]{1,0:T(8,128)(2,1)} async-done(((bf16[672,1024]{1,0:T(8,128)(2,1)}), bf16[5376,1024]{1,0:T(8,128)(2,1)}) %all-gather.10.cloned.1.call-update) | async-done | bytes 11010064 | tf_op jit(solution)/shard_map/all_gather | solution.py:71
  384.9 8.1 %convolution_bitcast_fusion = f32[32,8,8,128]{3,1,2,0:T(8,128)S(1)} fusion(bf16[5376,1024]{1,0:T(8,128)(2,1)} %all-gather.10.cloned.1.call-done, f32[5376]{0:T(1024)S(1)} %copy-done.8, f32[256]{0:T(256)S(1)} %add_rsqrt_fusion.3, bf16[256,10752]{0,1:T(8,128)(2,1)} %copy-done.1, s32[]{:T(128)S(6)} %select_n.26), kind=kOutput, calls=%fused_computation.27 | convolution fusion | flops 2824077312 | bytes 14833668 | tf_op jit(solution)/shard_map/dot_general | solution.py:67
  396.0 1.2 multiply_multiply_fusion
  397.2 1.3 multiply_subtract_fusion
  399.0 1.7 fusion
  400.7 1.8 fusion.1
  402.5 3.3 divide_convert_fusion
  405.9 142.4 %all-gather.14.cloned.1.call-done = bf16[4096,1344]{0,1:T(8,128)(2,1)} async-done(((bf16[512,1344]{0,1:T(8,128)(2,1)}), bf16[4096,1344]{0,1:T(8,128)(2,1)}) %all-gather.14.cloned.1.call-update) | async-done | bytes 11010064 | tf_op jit(solution)/shard_map/all_gather | solution.py:129
  548.2 22.2 %all-gather.12.cloned.1.call-done = bf16[256,4096]{0,1:T(8,128)(2,1)} async-done(((bf16[256,1024]{0,1:T(8,128)(2,1)}), bf16[256,4096]{0,1:T(8,128)(2,1)}) %all-gather.12.cloned.1.call-update) | async-done | bytes 2097168 | tf_op jit(solution)/shard_map/all_gather | solution.py:126
  570.5 6.4 %multiply_reduce_fusion = (f32[256]{0:T(256)S(1)}, f32[256,1344]{0,1:T(8,128)S(1)}) fusion(bf16[4096,1344]{0,1:T(8,128)(2,1)} %all-gather.14.cloned.1.call-done, bf16[256,4096]{0,1:T(8,128)(2,1)} %all-gather.12.cloned.1.call-done), kind=kOutput, calls=%fused_computation.25 | convolution fusion | flops 2819260160 | bytes 14484480 | tf_op jit(solution)/shard_map/dot_general | solution.py:127
  576.9 5.9 psum.7
  582.8 1.2 add_convert_fusion
  (63 shorter events, 11.0 us)
Async XLA Ops:
  6.5 35.0 %copy-start = (bf16[256,1344]{0,1:T(8,128)(2,1)S(1)}, bf16[256,1344]{0,1:T(8,128)(2,1)}, u32[]{:S(2)}) copy-start(bf16[256,1344]{0,1:T(8,128)(2,1)} %param.12) | copy-start | bytes 2064388
  6.5 95.2 %all-gather.6.cloned.1.call-start = ((), (), s32[]{:S(2)}) async-start(), calls=%async_computation | async-start | bytes 6193152 | tf_op jit(solution)/shard_map/all_gather | solution.py:69
  7.3 184.3 %all-gather.8.cloned.1.call-start = ((), (), s32[]{:S(2)}) async-start(), calls=%async_computation.1 | async-start | bytes 6193152 | tf_op jit(solution)/shard_map/all_gather | solution.py:70
  8.0 376.9 %all-gather.10.cloned.1.call-start = ((), (), s32[]{:S(2)}) async-start(), calls=%async_computation.2 | async-start | bytes 12386304 | tf_op jit(solution)/shard_map/all_gather | solution.py:71
  8.7 539.5 %all-gather.14.cloned.1.call-start = ((), (), s32[]{:S(2)}) async-start(), calls=%async_computation.4 | async-start | bytes 12386304 | tf_op jit(solution)/shard_map/all_gather | solution.py:129
  9.3 561.1 %all-gather.12.cloned.1.call-start = ((), (), s32[]{:S(2)}) async-start(), calls=%async_computation.3 | async-start | bytes 2621440 | tf_op jit(solution)/shard_map/all_gather | solution.py:126
  9.4 11.3 %collective-permute-start = (bf16[256,1344]{0,1:T(8,128)(2,1)}, bf16[256,1344]{0,1:T(8,128)(2,1)S(1)}, u32[]{:S(2)}, u32[]{:S(2)}) collective-permute-start(bf16[256,1344]{0,1:T(8,128)(2,1)} %param.12), channel_id=1, source_target_pairs={{0,8},{8,16},{16,24},{24,0},{1,9},{9,17},{17,25},{25,1},{2,10},{10... | collective-permute-start | bytes 2064392 | tf_op jit(solution)/shard_map/ppermute | solution.py:60
  20.6 10.4 %collective-permute-start.1 = (bf16[256,1344]{0,1:T(8,128)(2,1)S(1)}, bf16[256,1344]{0,1:T(8,128)(2,1)S(1)}, u32[]{:S(2)}, u32[]{:S(2)}) collective-permute-start(bf16[256,1344]{0,1:T(8,128)(2,1)S(1)} %collective-permute-done), channel_id=1, source_target_pairs={{0,8},{8,16},{16,24},{24,0},{1,9},{9,17},{17,25},{25,1},{2,10},{10... | collective-permute-start | bytes 2064392 | tf_op jit(solution)/shard_map/ppermute | solution.py:60
  31.0 10.4 %collective-permute-start.2 = (bf16[256,1344]{0,1:T(8,128)(2,1)S(1)}, bf16[256,1344]{0,1:T(8,128)(2,1)S(1)}, u32[]{:S(2)}, u32[]{:S(2)}) collective-permute-start(bf16[256,1344]{0,1:T(8,128)(2,1)S(1)} %collective-permute-done.1), channel_id=1, source_target_pairs={{0,8},{8,16},{16,24},{24,0},{1,9},{9,17},{17,25},{25,1},{2,10},{10... | collective-permute-start | bytes 2064392 | tf_op jit(solution)/shard_map/ppermute | solution.py:60
  32.2 77.0 %copy-start.3 = (f32[256,64]{1,0:T(8,128)}, f32[256,64]{1,0:T(8,128)S(1)}, u32[]{:S(2)}) copy-start(f32[256,64]{1,0:T(8,128)S(1)} %get-tuple-element.12) | copy-start | bytes 196612
  41.5 60.3 %copy-start.8 = (f32[5376]{0:T(1024)S(1)}, f32[5376]{0:T(1024)}, u32[]{:S(2)}) copy-start(f32[5376]{0:T(1024)} %param.13) | copy-start | bytes 64516
  41.8 2.4 copy-start.1
  45.2 63.6 %copy-start.6 = (f32[128]{0:T(128)S(1)}, f32[128]{0:T(128)}, u32[]{:S(2)}) copy-start(f32[128]{0:T(128)} %param.18) | copy-start | bytes 1540
  110.2 177.5 %copy-start.4 = (bf16[1024,512]{1,0:T(8,128)(2,1)S(1)}, bf16[1024,512]{1,0:T(8,128)(2,1)}, u32[]{:S(2)}) copy-start(bf16[1024,512]{1,0:T(8,128)(2,1)} %param.20) | copy-start | bytes 3145732
  198.2 24.1 %collective-permute-start.3 = (bf16[2,256,512]{2,1,0:T(8,128)(2,1)S(1)}, bf16[2,256,512]{2,1,0:T(8,128)(2,1)S(1)}, u32[]{:S(2)}, u32[]{:S(2)}) collective-permute-start(bf16[2,256,512]{2,1,0:T(8,128)(2,1)S(1)} %pad_maximum_fusion), channel_id=1, source_target_pairs={{0,1},{1,2},{2,3},{3,4},{4,5},{5,6},{6,7},{8,9},{9,10},{10,11},{11... | collective-permute-start | bytes 1572872 | tf_op jit(solution)/shard_map/ppermute | solution.py:16
  222.3 14.7 %collective-permute-start.4 = (bf16[2,256,512]{2,1,0:T(8,128)(2,1)S(1)}, bf16[2,256,512]{2,1,0:T(8,128)(2,1)}, u32[]{:S(2)}, u32[]{:S(2)}) collective-permute-start(bf16[2,256,512]{2,1,0:T(8,128)(2,1)S(1)} %collective-permute-done.3), channel_id=1, source_target_pairs={{0,1},{1,2},{2,3},{3,4},{4,5},{5,6},{6,7},{8,9},{9,10},{10,11},{11... | collective-permute-start | bytes 1572872 | tf_op jit(solution)/shard_map/ppermute | solution.py:16
  237.1 21.5 %collective-permute-start.5 = (bf16[2,256,512]{2,1,0:T(8,128)(2,1)}, bf16[2,256,512]{2,1,0:T(8,128)(2,1)}, u32[]{:S(2)}, u32[]{:S(2)}) collective-permute-start(bf16[2,256,512]{2,1,0:T(8,128)(2,1)} %collective-permute-done.4), channel_id=1, source_target_pairs={{0,1},{1,2},{2,3},{3,4},{4,5},{5,6},{6,7},{8,9},{9,10},{10,11},{11... | collective-permute-start | bytes 1572872 | tf_op jit(solution)/shard_map/ppermute | solution.py:16
  258.5 29.2 %collective-permute-start.6 = (bf16[2,256,512]{2,1,0:T(8,128)(2,1)}, bf16[2,256,512]{2,1,0:T(8,128)(2,1)S(1)}, u32[]{:S(2)}, u32[]{:S(2)}) collective-permute-start(bf16[2,256,512]{2,1,0:T(8,128)(2,1)} %collective-permute-done.5), channel_id=1, source_target_pairs={{0,1},{1,2},{2,3},{3,4},{4,5},{5,6},{6,7},{8,9},{9,10},{10,11},{11... | collective-permute-start | bytes 1572872 | tf_op jit(solution)/shard_map/ppermute | solution.py:16
  300.3 95.7 %copy-start.7 = (f32[128]{0:T(128)S(1)}, f32[128]{0:T(128)}, u32[]{:S(2)}) copy-start(f32[128]{0:T(128)} %param.17) | copy-start | bytes 1540
  400.7 1.8 copy-start.2
  405.9 177.0 %copy-start.5 = (f32[1344]{0:T(1024)S(1)}, f32[1344]{0:T(1024)}, u32[]{:S(2)}) copy-start(f32[1344]{0:T(1024)} %param.23) | copy-start | bytes 16132
Sparse Core Ops, SparseCore 0:
  9.5 92.1 all-gather.5
  103.9 87.6 all-gather.7
  193.8 191.0 all-gather.9
  386.8 161.3 all-gather.13
  549.6 20.7 all-gather.11
